TPU v7x, 256 devices: a whole 4x4x8 slice. The times are simulated.
256 devices in a mesh: dp: 16 (over z, y_hi), row: 4 (over y_lo, core), col: 4 (over x).
Axes of the slice: x: 4, y: 4 (y_hi: 2, y_lo: 2; y = y_hi * 2 + y_lo), z: 8, core: 2. Of those that a mesh axis runs over, the one named last changes fastest.
Arguments:
- tokens: bfloat16 [7168, 4096], P(('dp', 'col'), 'row'), may hold values from -6 to 6
- gate_up: bfloat16 [2, 4096, 14336], P(None, 'row', ('dp', 'col')), may hold values from -0.09375 to 0.09375
- down_weight: bfloat16 [14336, 4096], P(('dp', 'col'), 'row'), may hold values from -0.046875 to 0.046875
Outputs:
- mixed: bfloat16 [7168, 4096], P(('dp', 'col'), 'row')
- col_check: float32 [4096], P('row')
- row_check: float32 [7168], P(('dp', 'col'))
All inputs are finite; a program needn't handle non-finite values.
Results may differ from a plain program's by a relative error of at most 0.0049.
Values may be sent and summed in bfloat16 or wider, within the bound.
No kernel may reach another device: no remote copies, remote signals or barrier semaphores. Data moves between devices by JAX's collectives and lax.ppermute only.
A program may use at most 128 MiB of HBM per device.

v0:
```python
import math
import jax
import jax.numpy as jnp
from jax import lax
from jax.sharding import PartitionSpec as P


def swiglu(partial_value):
    return (jax.nn.silu(partial_value[:, 0]) * partial_value[:, 1]).astype(jnp.bfloat16)


def hidden_units(partial_value):
    share = lax.psum_scatter(partial_value, "row", scatter_dimension=0, tiled=True)
    return lax.all_gather(swiglu(share), "row", axis=0, tiled=True)


def make_accumulate(hidden, shard_piece):
    columns_wide = hidden.astype(jnp.float32)
    piece_wide = shard_piece.astype(jnp.float32)
    output_part = jnp.dot(hidden, shard_piece, preferred_element_type=jnp.float32)
    column_part = jnp.dot(
        jnp.sum(columns_wide, axis=0), piece_wide, precision=lax.Precision.HIGHEST
    )
    row_part = jnp.dot(columns_wide, jnp.sum(piece_wide, axis=1), precision=lax.Precision.HIGHEST)
    return (output_part, column_part, row_part)


def per_device(tokens, gate_up, down_weight):
    total_tokens = tokens.shape[0] * lax.axis_size(("dp", "col"))
    model_width = tokens.shape[1] * lax.axis_size("row")
    group_rows = lax.all_gather(tokens, "col", axis=0, tiled=True)
    partial_value = jnp.einsum(
        "td,gdf->tgf",
        group_rows,
        lax.all_gather(gate_up, "dp", axis=2, tiled=True),
        preferred_element_type=jnp.float32,
    )
    hidden = hidden_units(partial_value)
    output_part, column_part, row_part = make_accumulate(
        hidden, lax.all_gather(down_weight, "dp", axis=0, tiled=True)
    )
    mixed, row_share = (
        lax.psum_scatter(output_part, "col", scatter_dimension=0, tiled=True),
        lax.psum_scatter(row_part, "col", scatter_dimension=0, tiled=True),
    )
    col_check = lax.psum(column_part, ("dp", "col")) / math.sqrt(total_tokens)
    row_check = lax.psum(row_share, "row") / math.sqrt(model_width)
    return (mixed.astype(jnp.bfloat16), col_check, row_check)


def solution(mesh):
    placed = (P(("dp", "col"), "row"), P(None, "row", ("dp", "col")), P(("dp", "col"), "row"))
    return jax.shard_map(
        per_device,
        mesh=mesh,
        in_specs=placed,
        out_specs=(P(("dp", "col"), "row"), P("row"), P(("dp", "col"))),
        check_vma=False,
    )
```

profile of v0, /device:TPU:8, one launch (start us, length us, event | category | flops | bytes accessed | tf_op | source)
XLA Modules:
  0.0 748.7 jit_solution(9035475301600994231)
XLA Ops:
  7.2 0.0 all-gather.4.cloned.1.call-start
  7.2 0.7 all-gather.4.cloned.1.call-update
  7.9 0.0 reduce-scatter.3.cloned.1.call-start
  7.9 14.2 %all_gather.12 = bf16[448,1024]{1,0:T(8,128)(2,1)S(1)} all-gather(bf16[112,1024]{1,0:T(8,128)(2,1)} %param.3), channel_id=1, replica_groups=mesh['dp'=16,'row'=4,'col'=4] {'col'}, dimensions={0}, use_global_device_ids=true | all-gather | bytes 1146880 | tf_op jit(solution)/shard_map/all_gather | solution.py:31
  22.2 192.1 %all-gather.4.cloned.1.call-done = bf16[2,1024,3584]{1,2,0:T(8,128)(2,1)} async-done(((bf16[2,1024,224]{1,2,0:T(8,128)(2,1)}), bf16[2,1024,3584]{1,2,0:T(8,128)(2,1)}) %all-gather.4.cloned.1.call-update) | async-done | bytes 14680080 | tf_op jit(solution)/shard_map/all_gather | solution.py:35
  214.2 22.2 %fusion.2 = f32[448,2,3584]{2,0,1:T(8,128)} fusion(bf16[2,1024,3584]{1,2,0:T(8,128)(2,1)} %all-gather.4.cloned.1.call-done, bf16[448,1024]{1,0:T(8,128)(2,1)S(1)} %all_gather.12), kind=kOutput, calls=%fused_computation.6 | convolution fusion | flops 6576668672 | bytes 28442624 | tf_op jit(solution)/shard_map/td,gdf->tgf/dot_general | solution.py:32
  236.5 0.0 reduce-scatter.3.cloned.1.call-update
  236.5 0.0 all-gather.8.cloned.1.call-start
  236.5 0.7 all-gather.8.cloned.1.call-update
  237.2 0.0 all-gather.6.cloned.1.call-start
  237.3 113.1 %reduce-scatter.3.cloned.1.call-done = f32[112,2,3584]{2,0,1:T(8,128)} async-done(((f32[448,2,3584]{2,0,1:T(8,128)}), f32[112,2,3584]{2,0,1:T(8,128)}) %reduce-scatter.3.cloned.1.call-update) | async-done | bytes 3211280 | tf_op jit(solution)/shard_map/reduce_scatter | solution.py:13
  350.3 3.2 fusion.1
  353.6 0.0 all-gather.6.cloned.1.call-update
  353.6 0.0 copy-start.1
  353.6 0.0 reduce-scatter.5.cloned.1.call-start
  353.6 126.6 %all-gather.8.cloned.1.call-done = bf16[3584,1024]{1,0:T(8,128)(2,1)} async-done(((bf16[224,1024]{1,0:T(8,128)(2,1)}), bf16[3584,1024]{1,0:T(8,128)(2,1)}) %all-gather.8.cloned.1.call-update) | async-done | bytes 7340048 | tf_op jit(solution)/shard_map/all_gather | solution.py:40
  480.3 38.6 %all-gather.6.cloned.1.call-done = bf16[448,3584]{1,0:T(8,128)(2,1)} async-done(((bf16[112,3584]{1,0:T(8,128)(2,1)}), bf16[448,3584]{1,0:T(8,128)(2,1)}) %all-gather.6.cloned.1.call-update) | async-done | bytes 3211280 | tf_op jit(solution)/shard_map/all_gather | solution.py:14
  518.8 8.8 %fusion.4 = f32[448,1024]{1,0:T(8,128)} fusion(bf16[448,3584]{1,0:T(8,128)(2,1)} %all-gather.6.cloned.1.call-done, bf16[3584,1024]{1,0:T(8,128)(2,1)} %all-gather.8.cloned.1.call-done), kind=kOutput, calls=%fused_computation.10 | convolution fusion | flops 3288334336 | bytes 12386304 | tf_op jit(solution)/shard_map/dot_general | solution.py:20
  527.6 0.0 reduce-scatter.5.cloned.1.call-update
  527.6 0.0 copy-done.1
  527.6 0.6 dynamic-slice
  528.9 0.0 copy-start
  528.9 4.3 convert_reduce_fusion
  533.2 0.0 copy-done
  533.2 0.6 convert_reduce_fusion.1
  533.8 2.6 fusion.6
  536.4 10.9 %all-reduce = f32[448]{0:T(512)S(1)} all-reduce(f32[448]{0:T(512)S(1)} %bitcast.24), channel_id=4, replica_groups=mesh['dp'=16,'row'=4,'col'=4] {'col'}, use_global_device_ids=true, to_apply=%region_5.6.clone | all-reduce | flops 448 | bytes 3584
  547.2 0.1 dynamic-slice.1
  547.3 6.5 psum.15
  553.8 5.2 fusion.5
  559.0 180.3 %psum.14 = f32[1024]{0:T(1024)S(1)} all-reduce(f32[1024]{0:T(1024)S(1)} %bitcast.23), channel_id=1, replica_groups=mesh['dp'=16,'row'=4,'col'=4] {'dp','col'}, use_global_device_ids=true, to_apply=%region_3.4 | all-reduce | flops 1024 | bytes 8192 | tf_op jit(solution)/shard_map/psum | solution.py:46
  739.3 0.5 broadcast_multiply_fusion.1
  739.8 0.6 broadcast_multiply_fusion
  740.4 0.0 reduce-scatter.5.cloned.1.call-done
  740.4 1.7 convert_element_type.13
  (2 shorter events, 0.0 us)
Async XLA Ops:
  7.2 207.1 %all-gather.4.cloned.1.call-start = ((), (), s32[]{:S(2)}) async-start(), calls=%async_computation.2 | async-start | bytes 15597568 | tf_op jit(solution)/shard_map/all_gather | solution.py:35
  7.9 342.4 %reduce-scatter.3.cloned.1.call-start = ((), (), s32[]{:S(2)}) async-start(), calls=%async_computation.3 | async-start | bytes 16056320 | tf_op jit(solution)/shard_map/reduce_scatter | solution.py:13
  236.5 243.8 %all-gather.8.cloned.1.call-start = ((), (), s32[]{:S(2)}) async-start(), calls=%async_computation.5 | async-start | bytes 7798784 | tf_op jit(solution)/shard_map/all_gather | solution.py:40
  237.2 281.6 %all-gather.6.cloned.1.call-start = ((), (), s32[]{:S(2)}) async-start(), calls=%async_computation.4 | async-start | bytes 4014080 | tf_op jit(solution)/shard_map/all_gather | solution.py:14
  353.6 174.1 %copy-start.1 = (u32[256]{0:T(256)S(1)}, u32[256]{0:T(256)}, u32[]{:S(2)}) copy-start(u32[256]{0:T(256)} %constant.16) | copy-start | bytes 3076
  353.6 386.8 %reduce-scatter.5.cloned.1.call-start = ((), (), s32[]{:S(2)}) async-start(), calls=%async_computation.6 | async-start | bytes 2293760 | tf_op jit(solution)/shard_map/reduce_scatter | solution.py:43
  528.9 4.3 copy-start
Sparse Core Ops, SparseCore 0:
  10.6 203.5 all-gather.3
  236.6 113.6 reduce-scatter.2
  352.9 127.3 all-gather.7
  481.9 36.8 all-gather.5
  527.7 32.7 reduce-scatter.4
where the time goes:
time: 749 us
  waiting for transfers between devices  472 us (63%)
  blocking collectives  212 us (28%)
  matrix products  38.7 us (5%)
  between operations  14.5 us (2%)
  other arithmetic  10.9 us (1%)
    all_gather x1, waiting for transfers between devices, per_device(): lax.all_gather(gate_up, 'dp', axis=2, tiled=True)  192 us
    psum x1, blocking collectives, per_device(): col_check = lax.psum(column_part, ('dp', 'col')) / math.sqrt(total_tokens)  180 us
    all_gather x1, waiting for transfers between devices, per_device(): lax.all_gather(down_weight, 'dp', axis=0, tiled=True)  127 us
    reduce_scatter x1, waiting for transfers between devices, hidden_units(): lax.psum_scatter(partial_value, 'row', scatter_dimension=0, tiled=True)  113 us
    all_gather x1, waiting for transfers between devices, hidden_units(): return lax.all_gather(swiglu(share), 'row', axis=0, tiled=True)  38.6 us
    dot_general x1, matrix products, per_device(): jnp.einsum('td,gdf->tgf', group_rows, lax.all_gather(gate_up, 'dp', axis=...  22.2 us
  transfers between devices with their start and end apart: 5, of which 4 were waited for; matrix products, arithmetic and copies ran while one was open for 2% of the time, Pallas kernels for 0%

commit v1 on v0

--- a/solution.py
+++ b/solution.py
@@ -1,8 +1,18 @@
+import functools
 import math
 import jax
 import jax.numpy as jnp
 from jax import lax
 from jax.sharding import PartitionSpec as P
+
+
+def _raise_knots(payload, a_name, peer_axis):
+    for at in (a_name, peer_axis):
+        payload = lax.psum(payload, axis_name=at)
+    return payload
+
+
+fit_the_slot = functools.partial(_raise_knots, a_name="col", peer_axis="dp")
 
 
 def swiglu(partial_value):
@@ -43,7 +53,7 @@
         lax.psum_scatter(output_part, "col", scatter_dimension=0, tiled=True),
         lax.psum_scatter(row_part, "col", scatter_dimension=0, tiled=True),
     )
-    col_check = lax.psum(column_part, ("dp", "col")) / math.sqrt(total_tokens)
+    col_check = fit_the_slot(column_part) / math.sqrt(total_tokens)
     row_check = lax.psum(row_share, "row") / math.sqrt(model_width)
     return (mixed.astype(jnp.bfloat16), col_check, row_check)
 

time: 749 us -> 611 us (0.82)
  blocking collectives: 212 us -> 73.6 us
    psum x1 -> x2, blocking collectives: 180 us -> 52.8 us  [_raise_knots(): payload = lax.psum(payload, axis_name=at)]
    unnamed x1 -> x0, blocking collectives: 10.9 us -> none
  transfers between devices with their start and end apart: 5 -> 5, of which waited for: 4 -> 4; matrix products, arithmetic and copies ran while one was open for 2% -> 3% of each run, Pallas kernels for 0% -> 0%
where the time goes in v1:
time: 611 us
  waiting for transfers between devices  472 us (77%)
  blocking collectives  73.6 us (12%)
  matrix products  36.5 us (6%)
  between operations  14.8 us (2%)
  other arithmetic  13 us (2%)
    all_gather x1, waiting for transfers between devices, per_device(): lax.all_gather(gate_up, 'dp', axis=2, tiled=True)  192 us
    all_gather x1, waiting for transfers between devices, per_device(): lax.all_gather(down_weight, 'dp', axis=0, tiled=True)  126 us
    reduce_scatter x1, waiting for transfers between devices, hidden_units(): lax.psum_scatter(partial_value, 'row', scatter_dimension=0, tiled=True)  113 us
    psum x2, blocking collectives, _raise_knots(): payload = lax.psum(payload, axis_name=at)  52.8 us
    all_gather x1, waiting for transfers between devices, hidden_units(): return lax.all_gather(swiglu(share), 'row', axis=0, tiled=True)  38.6 us
    dot_general x1, matrix products, per_device(): jnp.einsum('td,gdf->tgf', group_rows, lax.all_gather(gate_up, 'dp', axis=...  22.2 us
    all_gather x1, blocking collectives, per_device(): group_rows = lax.all_gather(tokens, 'col', axis=0, tiled=True)  14.2 us
  transfers between devices with their start and end apart: 5, of which 4 were waited for; matrix products, arithmetic and copies ran while one was open for 3% of the time, Pallas kernels for 0%

profile of v1, /device:TPU:8, one launch (start us, length us, event | category | flops | bytes accessed | tf_op | source)
XLA Modules:
  0.0 610.7 jit_solution(9749235932446568716)
XLA Ops:
  7.2 0.0 all-gather.4.cloned.1.call-start
  7.2 0.7 all-gather.4.cloned.1.call-update
  7.9 0.0 reduce-scatter.3.cloned.1.call-start
  7.9 14.2 %all_gather.12 = bf16[448,1024]{1,0:T(8,128)(2,1)S(1)} all-gather(bf16[112,1024]{1,0:T(8,128)(2,1)} %param.3), channel_id=1, replica_groups=mesh['dp'=16,'row'=4,'col'=4] {'col'}, dimensions={0}, use_global_device_ids=true | all-gather | bytes 1146880 | tf_op jit(solution)/shard_map/all_gather | solution.py:41
  22.2 192.1 %all-gather.4.cloned.1.call-done = bf16[2,1024,3584]{1,2,0:T(8,128)(2,1)} async-done(((bf16[2,1024,224]{1,2,0:T(8,128)(2,1)}), bf16[2,1024,3584]{1,2,0:T(8,128)(2,1)}) %all-gather.4.cloned.1.call-update) | async-done | bytes 14680080 | tf_op jit(solution)/shard_map/all_gather | solution.py:45
  214.2 22.2 %fusion.2 = f32[448,2,3584]{2,0,1:T(8,128)} fusion(bf16[2,1024,3584]{1,2,0:T(8,128)(2,1)} %all-gather.4.cloned.1.call-done, bf16[448,1024]{1,0:T(8,128)(2,1)S(1)} %all_gather.12), kind=kOutput, calls=%fused_computation.6 | convolution fusion | flops 6576668672 | bytes 28442624 | tf_op jit(solution)/shard_map/td,gdf->tgf/dot_general | solution.py:42
  236.5 0.0 reduce-scatter.3.cloned.1.call-update
  236.5 0.0 all-gather.8.cloned.1.call-start
  236.6 0.7 all-gather.8.cloned.1.call-update
  237.2 0.0 all-gather.6.cloned.1.call-start
  237.3 113.1 %reduce-scatter.3.cloned.1.call-done = f32[112,2,3584]{2,0,1:T(8,128)} async-done(((f32[448,2,3584]{2,0,1:T(8,128)}), f32[112,2,3584]{2,0,1:T(8,128)}) %reduce-scatter.3.cloned.1.call-update) | async-done | bytes 3211280 | tf_op jit(solution)/shard_map/reduce_scatter | solution.py:23
  350.4 3.2 fusion.1
  353.6 0.0 all-gather.6.cloned.1.call-update
  353.6 0.0 copy-start.1
  353.6 0.2 reduce-scatter.5.cloned.1.call-start
  353.8 126.5 %all-gather.8.cloned.1.call-done = bf16[3584,1024]{1,0:T(8,128)(2,1)} async-done(((bf16[224,1024]{1,0:T(8,128)(2,1)}), bf16[3584,1024]{1,0:T(8,128)(2,1)}) %all-gather.8.cloned.1.call-update) | async-done | bytes 7340048 | tf_op jit(solution)/shard_map/all_gather | solution.py:50
  480.3 38.6 %all-gather.6.cloned.1.call-done = bf16[448,3584]{1,0:T(8,128)(2,1)} async-done(((bf16[112,3584]{1,0:T(8,128)(2,1)}), bf16[448,3584]{1,0:T(8,128)(2,1)}) %all-gather.6.cloned.1.call-update) | async-done | bytes 3211280 | tf_op jit(solution)/shard_map/all_gather | solution.py:24
  518.9 8.7 %fusion.4 = f32[448,1024]{1,0:T(8,128)} fusion(bf16[448,3584]{1,0:T(8,128)(2,1)} %all-gather.6.cloned.1.call-done, bf16[3584,1024]{1,0:T(8,128)(2,1)} %all-gather.8.cloned.1.call-done), kind=kOutput, calls=%fused_computation.10 | convolution fusion | flops 3288334336 | bytes 12386304 | tf_op jit(solution)/shard_map/dot_general | solution.py:30
  527.6 0.0 slice-start
  527.6 0.0 reduce-scatter.5.cloned.1.call-update
  527.7 0.0 copy-done.1
  527.7 0.6 dynamic-slice
  529.2 0.0 slice-start.1
  529.2 4.3 convert_reduce_fusion
  533.5 0.0 copy-start
  533.5 2.7 convert_reduce_fusion.1
  536.2 0.2 copy-done
  536.4 2.6 fusion.6
  538.9 0.0 slice-done
  538.9 0.0 slice-done.1
  539.0 2.9 fusion.5
  541.9 11.3 %all-reduce.1 = (f32[1024]{0:T(1024)S(1)}, f32[448]{0:T(512)S(1)}) all-reduce(f32[1024]{0:T(1024)S(1)} %bitcast.25, f32[448]{0:T(512)S(1)} %bitcast.26), channel_id=1, replica_groups=mesh['dp'=16,'row'=4,'col'=4] {'col'}, use_global_device_ids=true, to_apply=%region_3.4 | all-reduce | flops 1472 | bytes 11776 | tf_op jit(solution)/shard_map/psum | solution.py:11
  553.2 0.1 dynamic-slice.1
  553.3 6.5 %psum.23 = f32[112]{0:T(128)S(1)} all-reduce(f32[112]{0:T(128)S(1)} %dynamic-slice.1), channel_id=1, replica_groups=mesh['dp'=16,'row'=4,'col'=4] {'row'}, use_global_device_ids=true, to_apply=%region_7.8 | all-reduce | flops 112 | bytes 896 | tf_op jit(solution)/shard_map/psum | solution.py:57
  559.8 41.6 %psum.22 = f32[1024]{0:T(1024)S(1)} all-reduce(f32[1024]{0:T(1024)S(1)} %get-tuple-element.3), channel_id=1, replica_groups=mesh['dp'=16,'row'=4,'col'=4] {'dp'}, use_global_device_ids=true, to_apply=%region_4.5 | all-reduce | flops 1024 | bytes 8192 | tf_op jit(solution)/shard_map/psum | solution.py:11
  601.3 0.5 broadcast_multiply_fusion.1
  601.8 0.6 broadcast_multiply_fusion
  602.4 0.0 reduce-scatter.5.cloned.1.call-done
  602.4 1.7 convert_element_type.13
  (3 shorter events, 0.0 us)
Async XLA Ops:
  7.2 207.1 %all-gather.4.cloned.1.call-start = ((), (), s32[]{:S(2)}) async-start(), calls=%async_computation.2 | async-start | bytes 15597568 | tf_op jit(solution)/shard_map/all_gather | solution.py:45
  7.9 342.5 %reduce-scatter.3.cloned.1.call-start = ((), (), s32[]{:S(2)}) async-start(), calls=%async_computation.3 | async-start | bytes 16056320 | tf_op jit(solution)/shard_map/reduce_scatter | solution.py:23
  236.5 243.8 %all-gather.8.cloned.1.call-start = ((), (), s32[]{:S(2)}) async-start(), calls=%async_computation.5 | async-start | bytes 7798784 | tf_op jit(solution)/shard_map/all_gather | solution.py:50
  237.2 281.6 %all-gather.6.cloned.1.call-start = ((), (), s32[]{:S(2)}) async-start(), calls=%async_computation.4 | async-start | bytes 4014080 | tf_op jit(solution)/shard_map/all_gather | solution.py:24
  353.6 174.0 %copy-start.1 = (u32[256]{0:T(256)S(1)}, u32[256]{0:T(256)}, u32[]{:S(2)}) copy-start(u32[256]{0:T(256)} %constant.16) | copy-start | bytes 3076
  353.6 248.8 %reduce-scatter.5.cloned.1.call-start = ((), (), s32[]{:S(2)}) async-start(), calls=%async_computation.6 | async-start | bytes 2293760 | tf_op jit(solution)/shard_map/reduce_scatter | solution.py:53
  527.6 11.3 %slice-start = ((s8[7340032]{0:T(1024)(128)(4,1)}), s8[3145728]{0:T(1024)(128)(4,1)S(1)}, s32[]{:S(2)}) async-start(s8[7340032]{0:T(1024)(128)(4,1)} %bitcast.23), calls=%async_computation.7 | async-start | bytes 6291456
  529.2 9.7 %slice-start.1 = ((s8[7340032]{0:T(1024)(128)(4,1)}), s8[4194304]{0:T(1024)(128)(4,1)S(1)}, s32[]{:S(2)}) async-start(s8[7340032]{0:T(1024)(128)(4,1)} %bitcast.23), calls=%async_computation.8 | async-start | bytes 8388608
  533.5 2.9 copy-start
Sparse Core Ops, SparseCore 0:
  10.6 203.5 all-gather.3
  236.6 113.6 reduce-scatter.2
  352.9 127.3 all-gather.7
  482.0 36.8 all-gather.5
  527.8 33.0 reduce-scatter.4
